TPU v7x, 32 devices: a whole 2x2x4 slice. The times are simulated.
32 devices in a mesh: groups: 2 (over x), pb: 16 (over z, y, core).
Axes of the slice: x: 2, y: 2, z: 4, core: 2. Of those that a mesh axis runs over, the one named last changes fastest.
Arguments:
- eigvec: bfloat16 [8192, 2592], P(('groups', 'pb')), parts along dimension 0, may hold values from -0.69921875 to 0.69921875
- omega: bfloat16 [8192, 36], P(('groups', 'pb')), parts along dimension 0, may hold values from 0.5 to 4
- phi: bfloat16 [36, 36, 36], replicated, may hold values from -6 to 6
- send_rows: int32 [32, 32], P(('groups', 'pb')), parts along dimension 0, may hold values from 0 to 255
- local_q: int32 [512], P(('groups', 'pb')), parts along dimension 0, may hold values from 0 to 255
- partner_q: int32 [512], P(('groups', 'pb')), parts along dimension 0, may hold values from 0 to 255
- slot_ref: int32 [512], P(('groups', 'pb')), parts along dimension 0, may hold values from 0 to 31, as said below
- tri_count: int32 [32], P(('groups', 'pb')), parts along dimension 0, may hold values from 8 to 16, as said below
Outputs:
- rates: float32 [36, 8192], P(None, ('groups', 'pb')), parts along dimension 1
There are 2 independent parts, one for each index of `groups`. A program takes and returns all parts, laid end to end along the dimension named above; an argument that names none is the same for every part. Nothing has to cross between parts.
Inputs may be any that keep to these rules, and one draw needn't show every extreme that they name: slot_ref of a live triplet of device p names an owner o and a slot s below the number of slots that o fills for p, which is 1 to 2; each device receives 2 filled slots from some owner. `tri_count`: exactly one device has 16 live triplets; live triplets come first.
All inputs are finite; a program needn't handle non-finite values.
Results may differ from a plain program's by a relative error of at most 0.00048.
Values may be sent and summed in bfloat16 or wider, within the bound.
A program may use at most 128 MiB of HBM per device.

v0:
```python
import jax
import jax.numpy as jnp
from jax import lax
from jax.sharding import PartitionSpec as P

NB = 36
BLK = 16


smear_width = 0.5


def triplet_rates(
    phi, near_vec, partner_vec, far_vec, near_freq, partner_freq, far_freq, weight_mask
):
    y_real = jnp.einsum("abc,tnc->tabn", phi, far_vec[:, 0], preferred_element_type=jnp.float32)
    y_imag = -jnp.einsum("abc,tnc->tabn", phi, far_vec[:, 1], preferred_element_type=jnp.float32)
    y_real = y_real.astype(jnp.bfloat16)
    y_imag = y_imag.astype(jnp.bfloat16)
    part_real = partner_vec[:, 0]
    part_imag = partner_vec[:, 1]
    z_real = jnp.einsum(
        "tmb,tabn->tamn", part_real, y_real, preferred_element_type=jnp.float32
    ) - jnp.einsum("tmb,tabn->tamn", part_imag, y_imag, preferred_element_type=jnp.float32)
    z_imag = jnp.einsum(
        "tmb,tabn->tamn", part_real, y_imag, preferred_element_type=jnp.float32
    ) + jnp.einsum("tmb,tabn->tamn", part_imag, y_real, preferred_element_type=jnp.float32)
    z_real = z_real.astype(jnp.bfloat16)
    z_imag = z_imag.astype(jnp.bfloat16)
    near_real = near_vec[:, 0]
    near_imag = near_vec[:, 1]
    v_real = jnp.einsum(
        "tva,tamn->tvmn", near_real, z_real, preferred_element_type=jnp.float32
    ) - jnp.einsum("tva,tamn->tvmn", near_imag, z_imag, preferred_element_type=jnp.float32)
    v_imag = jnp.einsum(
        "tva,tamn->tvmn", near_real, z_imag, preferred_element_type=jnp.float32
    ) + jnp.einsum("tva,tamn->tvmn", near_imag, z_real, preferred_element_type=jnp.float32)
    power = v_real * v_real + v_imag * v_imag
    first = near_freq.astype(jnp.float32)[:, :, None, None]
    second = partner_freq.astype(jnp.float32)[:, None, :, None]
    third = far_freq.astype(jnp.float32)[:, None, None, :]
    offset = (first + second - third) / smear_width
    weight = jnp.exp(-offset * offset) / (first * second * third * NB)
    terms = power * weight * weight_mask[:, None, None, None]
    return (jnp.sum(terms, axis=(2, 3)), jnp.sum(terms, axis=(1, 2)))


def on_device(eigvec, omega, phi, send_rows, local_q, partner_q, slot_ref, tri_count):
    owned = eigvec.shape[0]
    outgoing = send_rows[0]
    sent_vec = jnp.take(eigvec, outgoing, axis=0)
    sent_freq = jnp.take(omega, outgoing, axis=0)
    far_vecs, far_freqs = (
        lax.all_to_all(sent_vec, "pb", split_axis=0, concat_axis=0, tiled=True),
        lax.all_to_all(sent_freq, "pb", split_axis=0, concat_axis=0, tiled=True),
    )
    live = tri_count[0]
    tri_slots = local_q.shape[0]
    empty = jnp.zeros((tri_slots, NB), jnp.float32)

    def one_block(block, carry):
        start = block * BLK
        weight_mask = (start + jnp.arange(BLK, dtype=jnp.int32) < live).astype(jnp.float32)
        near_vec = jnp.take(eigvec, local_q, axis=0).reshape(BLK, 2, NB, NB)
        partner_vec = jnp.take(eigvec, partner_q, axis=0).reshape(BLK, 2, NB, NB)
        far_vec = jnp.take(far_vecs, slot_ref, axis=0).reshape(BLK, 2, NB, NB)
        near_part, far_part = triplet_rates(
            phi,
            near_vec,
            partner_vec,
            far_vec,
            jnp.take(omega, local_q, axis=0),
            jnp.take(omega, partner_q, axis=0),
            jnp.take(far_freqs, slot_ref, axis=0),
            weight_mask,
        )
        return (near_part, far_part)

    upper = (live + BLK - 1) // BLK
    near_terms, far_terms = lax.fori_loop(0, upper, one_block, (empty, empty))
    by_slot = jnp.zeros((NB, outgoing.shape[0]), jnp.float32)
    by_slot = by_slot.at[:, slot_ref].add(far_terms.T)
    returned = lax.all_to_all(by_slot, "pb", split_axis=1, concat_axis=1, tiled=True)
    rates = jnp.zeros((NB, owned), jnp.float32)
    rates = rates.at[:, local_q].add(near_terms.T)
    rates = rates.at[:, outgoing].add(returned)
    return rates


def solution(mesh):
    in_specs = (
        P(("groups", "pb"), None),
        P(("groups", "pb"), None),
        P(),
        P(("groups", "pb"), None),
        P(("groups", "pb")),
        P(("groups", "pb")),
        P(("groups", "pb")),
        P(("groups", "pb")),
    )
    out_specs = P(None, ("groups", "pb"))
    return jax.shard_map(
        on_device, mesh=mesh, in_specs=in_specs, out_specs=out_specs, check_vma=False
    )
```

profile of v0, /device:TPU:0, one launch (start us, length us, event | category | flops | bytes accessed | tf_op | source)
XLA Modules:
  0.0 156.0 jit_solution(6795776041242217636)
XLA Ops:
  0.0 0.7 fusion.20
  0.7 0.5 broadcast.273
  1.2 1.3 reduce.3
  2.5 0.0 copy-done.2
  2.5 0.1 squeeze.45
  2.6 0.9 copy.32
  3.5 0.6 gather_fusion.2
  4.1 0.7 broadcast_select_fusion.3
  4.7 7.4 %all-to-all-start.1 = ((bf16[16,2,36]{2,1,0:T(2,128)(2,1)}), bf16[16,2,36]{2,1,0:T(2,128)(2,1)S(1)}, u32[]{:S(2)}, u32[]{:S(2)}) async-start(bf16[16,2,36]{2,1,0:T(2,128)(2,1)} %broadcast_select_fusion.3), calls=%async_computation.1 | async-start | bytes 16384 | tf_op jit(solution)/shard_map/all_to_all | solution.py:55
  12.2 0.7 compare_and_fusion.2
  12.8 0.7 compare_select_fusion.5
  13.5 0.7 compare_and_fusion.3
  14.2 0.7 compare_select_fusion.2
  14.8 1.8 %copy.29 = bf16[256,2592]{1,0:T(8,128)(2,1)S(1)} copy(bf16[256,2592]{0,1:T(8,128)(2,1)} %param.14) | data formatting | bytes 2654208 | tf_op args[0]
  16.6 0.0 copy-done.4
  16.6 0.7 gather_fusion
  17.3 0.6 gather_fusion.5
  17.9 0.6 gather_fusion.4
  18.5 0.1 gather.35
  18.6 0.9 broadcast_select_fusion
  19.5 0.1 broadcast_select_fusion.1
  19.6 0.7 compare_select_fusion.3
  20.9 0.6 gather_fusion.7
  21.5 0.6 gather_fusion.6
  22.1 0.0 all-to-all-done.1
  22.1 6.0 %all-to-all-start = ((bf16[16,2,2592]{2,1,0:T(2,128)(2,1)}), bf16[16,2,2592]{2,1,0:T(2,128)(2,1)S(1)}, u32[]{:S(2)}, u32[]{:S(2)}) async-start(bf16[16,2,2592]{2,1,0:T(2,128)(2,1)} %broadcast_select_fusion), calls=%async_computation | async-start | bytes 344064 | tf_op jit(solution)/shard_map/all_to_all | solution.py:54
  28.1 0.1 broadcast_select_fusion.4
  28.2 0.6 gather_fusion.3
  28.8 7.9 %all-to-all-done = bf16[16,2,2592]{2,1,0:T(2,128)(2,1)S(1)} async-done(((bf16[16,2,2592]{2,1,0:T(2,128)(2,1)}), bf16[16,2,2592]{2,1,0:T(2,128)(2,1)S(1)}, u32[]{:S(2)}, u32[]{:S(2)}) %all-to-all-start) | async-done | bytes 165920 | tf_op jit(solution)/shard_map/all_to_all | solution.py:54
  36.7 0.1 all_to_all.21
  36.8 0.6 gather_fusion.1
  37.4 0.6 broadcast_in_dim.78.clone
  38.0 0.6 broadcast_in_dim.78
  38.6 0.0 copy-done.5
  38.6 104.5 %while.15 = (s32[]{:T(128)}, f32[16,36]{1,0:T(8,128)}, f32[16,36]{1,0:T(8,128)}, s32[]{:T(128)}, s32[16]{0:T(128)}, /*index=5*/bf16[16,2592]{1,0:T(8,128)(2,1)S(...) while((s32[]{:T(128)}, f32[16,36]{1,0:T(8,128)}, ...), condition=%wide.region_3.6_spmd, body=%wide.region_0.5_spmd.sunk | while | flops 554730752 | bytes 99940664 | solution.py:80
  38.7 1.3 compare_convert_fusion.2
  40.0 0.1 select_convert_fusion.2
  40.0 0.4 reshape.252
  40.5 0.4 reshape.251
  40.9 0.4 gather.63
  41.3 0.1 copy_select_fusion.2
  41.4 0.1 broadcast_add_fusion.2
  41.5 5.2 %fusion.58 = bf16[16,36,36,36]{2,3,1,0:T(8,128)(2,1)} fusion(bf16[36,36,36]{2,1,0:T(8,128)(2,1)} %get-tuple-element.391, bf16[16,2,36,36]{3,2,0,1:T(8,128)(2,1)S(1)} %copy_select_fusion.2), kind=kOutput, calls=%fused_computation.19.clone.1 | convolution fusion | flops 55240704 | bytes 1750144 | tf_op jit(solution)/shard_map/while/body/abc,tnc->tabn/dot_general | solution.py:17
  46.8 2.7 %convolution_convert_fusion.2 = bf16[16,36,36,36]{3,1,2,0:T(8,128)(2,1)S(1)} fusion(bf16[36,36,36]{2,1,0:T(8,128)(2,1)} %get-tuple-element.391, bf16[16,2,36,36]{3,2,0,1:T(8,128)(2,1)S(1)} %copy_select_fusion.2), kind=kOutput, calls=%fused_computation.26.clone.1 | convolution fusion | flops 54494208 | bytes 1750144 | tf_op jit(solution)/shard_map/while/body/abc,tnc->tabn/dot_general | solution.py:16
  49.5 0.0 copy-start
  49.5 2.5 %copy-done = bf16[16,36,36,36]{3,1,2,0:T(8,128)(2,1)} copy-done((bf16[16,36,36,36]{3,1,2,0:T(8,128)(2,1)}, bf16[16,36,36,36]{3,1,2,0:T(8,128)(2,1)S(1)}, u32[]{:S(2)}) %copy-start) | copy-done | bytes 1493016 | tf_op jit(solution)/shard_map/while
  52.0 5.3 %fusion.61 = f32[16,36,36,36]{3,2,1,0:T(8,128)} fusion(bf16[16,36,36,36]{3,1,2,0:T(8,128)(2,1)S(1)} %convolution_convert_fusion.2, bf16[16,2,36,36]{3,2,1,0:T(8,128)(2,1)S(1)} %reshape.251), kind=kOutput, calls=%fused_computation.24.clone.1 | convolution fusion | flops 53747712 | bytes 9048064 | tf_op jit(solution)/shard_map/while/body/tmb,tabn->tamn/dot_general | solution.py:22
  57.3 10.2 %fusion.62 = bf16[16,36,36,36]{2,3,1,0:T(8,128)(2,1)} fusion(f32[16,36,36,36]{3,2,1,0:T(8,128)} %fusion.61, bf16[16,36,36,36]{2,3,1,0:T(8,128)(2,1)} %fusion.58, bf16[16,2,36,36]{3,2,1,0:T(8,128)(2,1)S(1)} %reshape.251), kind=kOutput, calls=%fused_computation.20.clone.1 | convolution fusion | flops 55240704 | bytes 6135808 | tf_op jit(solution)/shard_map/while/body/tmb,tabn->tamn/dot_general | solution.py:24
  67.5 9.9 %copy.52 = bf16[16,36,36,36]{1,3,2,0:T(8,128)(2,1)} copy(bf16[16,36,36,36]{2,3,1,0:T(8,128)(2,1)} %fusion.62) | data formatting | bytes 2985984 | tf_op jit(solution)/shard_map/while/body/convert_element_type | solution.py:28
  77.4 8.7 %fusion.57 = f32[16,36,36,36]{3,2,1,0:T(8,128)} fusion(bf16[16,36,36,36]{3,1,2,0:T(8,128)(2,1)} %copy-done, bf16[16,2,36,36]{3,2,1,0:T(8,128)(2,1)S(1)} %reshape.251), kind=kOutput, calls=%fused_computation.22.clone.1 | convolution fusion | flops 53747712 | bytes 4642816 | tf_op jit(solution)/shard_map/while/body/tmb,tabn->tamn/dot_general | solution.py:27
  86.1 10.3 %fusion.59 = bf16[16,36,36,36]{2,3,1,0:T(8,128)(2,1)} fusion(f32[16,36,36,36]{3,2,1,0:T(8,128)} %fusion.57, bf16[16,36,36,36]{2,3,1,0:T(8,128)(2,1)} %fusion.58, bf16[16,2,36,36]{3,2,1,0:T(8,128)(2,1)S(1)} %reshape.251), kind=kOutput, calls=%fused_computation.21.clone.1 | convolution fusion | flops 55240704 | bytes 6135808 | tf_op jit(solution)/shard_map/while/body/tmb,tabn->tamn/dot_general | solution.py:25
  96.4 9.9 %copy.51 = bf16[16,36,36,36]{1,3,2,0:T(8,128)(2,1)} copy(bf16[16,36,36,36]{2,3,1,0:T(8,128)(2,1)} %fusion.59) | data formatting | bytes 2985984 | tf_op jit(solution)/shard_map/while/body/convert_element_type | solution.py:29
  106.2 8.9 %fusion.64 = f32[16,36,36,36]{3,2,1,0:T(8,128)} fusion(bf16[16,36,36,36]{1,3,2,0:T(8,128)(2,1)} %copy.51, bf16[16,2,36,36]{3,2,1,0:T(8,128)(2,1)S(1)} %reshape.252), kind=kOutput, calls=%fused_computation.40.clone.1 | convolution fusion | flops 53747712 | bytes 4642816 | tf_op jit(solution)/shard_map/while/body/tva,tamn->tvmn/dot_general | solution.py:34
  115.1 0.0 copy-done.1
  115.1 5.2 %fusion.60 = f32[16,36,36,36]{3,2,1,0:T(8,128)} fusion(bf16[16,36,36,36]{1,3,2,0:T(8,128)(2,1)S(1)} %copy-done.1, bf16[16,2,36,36]{3,2,1,0:T(8,128)(2,1)S(1)} %reshape.252), kind=kOutput, calls=%fused_computation.38.clone.1 | convolution fusion | flops 53747712 | bytes 9048064 | tf_op jit(solution)/shard_map/while/body/tva,tamn->tvmn/dot_general | solution.py:35
  120.3 0.0 slice-done.1
  120.3 5.2 %fusion.63 = f32[16,36,36,36]{3,2,1,0:T(8,128)} fusion(bf16[16,36,36,36]{1,3,2,0:T(8,128)(2,1)S(1)} %bitcast.133, bf16[16,2,36,36]{3,2,1,0:T(8,128)(2,1)S(1)} %reshape.252), kind=kOutput, calls=%fused_computation.39.clone.1 | convolution fusion | flops 53747712 | bytes 9048064 | tf_op jit(solution)/shard_map/while/body/tva,tamn->tvmn/dot_general | solution.py:32
  125.5 17.6 %fusion.65 = (f32[16,36]{1,0:T(8,128)}, f32[16,36]{1,0:T(8,128)}) fusion(f32[16]{0:T(128)S(1)} %get-tuple-element.349, f32[16,36,36]{1,2,0:T(8,128)S(1)} %get-tuple-element.350, f32[16,36]{1,0:T(8,128)S(1)} %select_convert_fusion.2, f32[16,36,36]{1,2,0:T(8,128)S(1)} %get-tuple-element.352, f32[16,36,36,36]{3,2,1,0:T(8,128)} %fusion.60, ...), kind=kOutput, calls=%fused_computation.68.clone.1 | convolution fusion | flops 65690496 | bytes 11283456 | tf_op jit(solution)/shard_map/while/body/tva,tamn->tvmn/dot_general | solution.py:37
  143.2 1.4 scatter_custom_fusion.1
  144.5 3.5 %all-to-all-start.2 = ((f32[36,16,2]{0,2,1:T(2,128)}), f32[36,16,2]{0,2,1:T(2,128)S(1)}, u32[]{:S(2)}, u32[]{:S(2)}) async-start(f32[36,16,2]{0,2,1:T(2,128)} %bitcast.33), calls=%async_computation.2 | async-start | bytes 32768 | tf_op jit(solution)/shard_map/all_to_all | solution.py:83
  148.0 0.9 scatter_custom_fusion
  148.9 5.6 %all-to-all-done.2 = f32[36,16,2]{0,2,1:T(2,128)S(1)} async-done(((f32[36,16,2]{0,2,1:T(2,128)}), f32[36,16,2]{0,2,1:T(2,128)S(1)}, u32[]{:S(2)}, u32[]{:S(2)}) %all-to-all-start.2) | async-done | bytes 4640 | tf_op jit(solution)/shard_map/all_to_all | solution.py:83
  154.5 0.8 scatter_fusion
  155.3 0.7 copy.35
  (17 shorter events, 0.1 us)
Async XLA Ops:
  0.7 1.8 %copy-start.2 = (s32[32]{0:T(128)}, s32[32]{0:T(128)S(1)}, u32[]{:S(2)}) copy-start(s32[32]{0:T(128)S(1)} %fusion.20) | copy-start | bytes 388
  4.7 17.3 %all-to-all-start.1 = ((bf16[16,2,36]{2,1,0:T(2,128)(2,1)}), bf16[16,2,36]{2,1,0:T(2,128)(2,1)S(1)}, u32[]{:S(2)}, u32[]{:S(2)}) async-start(bf16[16,2,36]{2,1,0:T(2,128)(2,1)} %broadcast_select_fusion.3), calls=%async_computation.1 | async-start | bytes 16384 | tf_op jit(solution)/shard_map/all_to_all | solution.py:55
  13.5 3.1 %copy-start.4 = (s32[16]{0:T(128)}, s32[16]{0:T(128)S(1)}, u32[]{:S(2)}) copy-start(s32[16]{0:T(128)S(1)} %compare_select_fusion.5) | copy-start | bytes 196
  20.3 18.4 %copy-start.5 = (s32[16]{0:T(128)}, s32[16]{0:T(128)S(1)}, u32[]{:S(2)}) copy-start(s32[16]{0:T(128)S(1)} %compare_select_fusion.3) | copy-start | bytes 196
  22.1 14.6 %all-to-all-start = ((bf16[16,2,2592]{2,1,0:T(2,128)(2,1)}), bf16[16,2,2592]{2,1,0:T(2,128)(2,1)S(1)}, u32[]{:S(2)}, u32[]{:S(2)}) async-start(bf16[16,2,2592]{2,1,0:T(2,128)(2,1)} %broadcast_select_fusion), calls=%async_computation | async-start | bytes 344064 | tf_op jit(solution)/shard_map/all_to_all | solution.py:54
  38.6 115.9 %copy-start.3 = (s32[32]{0:T(128)S(1)}, s32[32]{0:T(128)}, u32[]{:S(2)}) copy-start(s32[32]{0:T(128)} %copy-done.2) | copy-start | bytes 388
  49.5 2.5 %copy-start = (bf16[16,36,36,36]{3,1,2,0:T(8,128)(2,1)}, bf16[16,36,36,36]{3,1,2,0:T(8,128)(2,1)S(1)}, u32[]{:S(2)}) copy-start(bf16[16,36,36,36]{3,1,2,0:T(8,128)(2,1)S(1)} %convolution_convert_fusion.2) | copy-start | bytes 4478980 | tf_op jit(solution)/shard_map/while
  106.2 8.9 %copy-start.1 = (bf16[16,36,36,36]{1,3,2,0:T(8,128)(2,1)S(1)}, bf16[16,36,36,36]{1,3,2,0:T(8,128)(2,1)}, u32[]{:S(2)}) copy-start(bf16[16,36,36,36]{1,3,2,0:T(8,128)(2,1)} %copy.51) | copy-start | bytes 4478980 | tf_op jit(solution)/shard_map/while
  106.2 14.1 %slice-start = ((s8[5898240]{0:T(1024)(128)(4,1)}), s8[4194304]{0:T(1024)(128)(4,1)S(1)}, s32[]{:S(2)}) async-start(s8[5898240]{0:T(1024)(128)(4,1)} %bitcast.132), calls=%async_computation.3 | async-start | bytes 8388608 | tf_op jit(solution)/shard_map/while
  115.1 5.2 %slice-start.1 = ((s8[5898240]{0:T(1024)(128)(4,1)}), s8[1703936]{0:T(1024)(128)(4,1)S(1)}, s32[]{:S(2)}) async-start(s8[5898240]{0:T(1024)(128)(4,1)} %bitcast.132), calls=%async_computation.4 | async-start | bytes 3407872 | tf_op jit(solution)/shard_map/while
  144.5 10.0 %all-to-all-start.2 = ((f32[36,16,2]{0,2,1:T(2,128)}), f32[36,16,2]{0,2,1:T(2,128)S(1)}, u32[]{:S(2)}, u32[]{:S(2)}) async-start(f32[36,16,2]{0,2,1:T(2,128)} %bitcast.33), calls=%async_computation.2 | async-start | bytes 32768 | tf_op jit(solution)/shard_map/all_to_all | solution.py:83
where the time goes:
time: 157 us; the launch traced here: 156 us
  matrix products  79.3 us (51%)
  local copies, waits for them, and re-layouts  33.6 us (21%)
  starting transfers between devices  16.9 us (11%)
  waiting for transfers between devices  13.5 us (9%)
  other arithmetic  11.7 us (7%)
    dot_general x1, matrix products, triplet_rates(): jnp.einsum('tva,tamn->tvmn', near_imag, z_real, preferred_element_type=jn...  17.6 us
    dot_general x1, matrix products, triplet_rates(): jnp.einsum('tmb,tabn->tamn', part_real, y_imag, preferred_element_type=jn...  10.3 us
    dot_general x1, matrix products, triplet_rates(): jnp.einsum('tmb,tabn->tamn', part_imag, y_imag, preferred_element_type=jn...  10.2 us
    convert_element_type x1, local copies, waits for them, and re-layouts, triplet_rates(): z_imag = z_imag.astype(jnp.bfloat16)  9.87 us
    convert_element_type x1, local copies, waits for them, and re-layouts, triplet_rates(): z_real = z_real.astype(jnp.bfloat16)  9.85 us
    dot_general x1, matrix products, triplet_rates(): jnp.einsum('tva,tamn->tvmn', near_imag, z_imag, preferred_element_type=jn...  8.89 us
    dot_general x1, matrix products, triplet_rates(): jnp.einsum('tmb,tabn->tamn', part_imag, y_real, preferred_element_type=jn...  8.74 us
    all_to_all x1, waiting for transfers between devices, on_device(): lax.all_to_all(sent_vec, 'pb', split_axis=0, concat_axis=0, tiled=True)  7.9 us
  transfers between devices with their start and end apart: 3, of which 2 were waited for; matrix products, arithmetic and copies ran while one was open for 7% of the time, Pallas kernels for 0%

commit v1 on v0

v1 whole, which is shorter than its diff:
```python
import functools

import jax
import jax.numpy as jnp
import numpy as np
from jax import lax
from jax.experimental import pallas as pl
from jax.experimental.pallas import tpu as pltpu
from jax.sharding import PartitionSpec as P

NB = 36
ROWS = 40
WIDE = 256
GROUPS = 6
smear_width = 0.5
F32, BF16 = jnp.float32, jnp.bfloat16
EXACT = lax.Precision.HIGHEST


def tables():
    start = [128 * h + 40 * u for h in range(2) for u in range(3)]
    spread_b = np.zeros((WIDE, NB), np.float32)
    spread_a = np.zeros((WIDE, NB), np.float32)
    pick = np.zeros((ROWS, WIDE), np.float32)
    own_two = np.full((WIDE,), -1)
    own_three = np.full((WIDE,), -2)
    column_two = np.full((WIDE,), -3)
    inner = np.full((WIDE,), -4)
    for block in range(GROUPS):
        for lane in range(NB):
            at = start[block] + lane
            outer, low = lane // GROUPS, lane % GROUPS
            spread_b[at, lane] = 1
            own_two[at] = block
            column_two[at] = outer
            spread_a[at, block * GROUPS + outer] = 1
            own_three[at] = low
            inner[at] = low
    for block in range(GROUPS):
        for lane in range(NB):
            pick[block * GROUPS + lane % GROUPS, start[block] + lane] = 1
    by_first = spread_a.T.copy()
    mask_two = (own_two[:, None] == column_two[None, :]).astype(np.float32)
    mask_three = (own_three[:, None] == inner[None, :]).astype(np.float32)
    second = np.zeros((GROUPS, NB, WIDE), np.float32)
    for group in range(GROUPS):
        for at in range(WIDE):
            if inner[at] >= 0:
                second[group, group * GROUPS + inner[at], at] = 1
    both_two = np.zeros((2 * ROWS, 2 * WIDE), np.float32)
    both_two[:ROWS, :WIDE] = pick
    both_two[ROWS:, WIDE:] = pick
    both_three = np.zeros((2 * ROWS, 2 * WIDE), np.float32)
    both_three[:NB, :WIDE] = by_first
    both_three[ROWS : ROWS + NB, WIDE:] = by_first
    by_first_rows = np.zeros((ROWS, WIDE), np.float32)
    by_first_rows[:NB] = by_first
    eye = np.zeros((ROWS, NB), np.float32)
    eye[:NB] = np.eye(NB)
    return dict(
        spread_b=spread_b.astype(BF16),
        spread_a=spread_a.astype(BF16),
        both_two=both_two.astype(BF16),
        both_three=both_three.astype(BF16),
        mask_two=mask_two,
        mask_three=mask_three,
        first=by_first.astype(BF16),
        second=np.transpose(second, (1, 0, 2)).reshape(NB, GROUPS * WIDE).astype(BF16),
        first_rows=by_first_rows,
        eye=eye.astype(BF16),
    )


NAMES = (
    "spread_b", "spread_a", "both_two", "both_three", "mask_two",
    "mask_three", "first", "second", "first_rows", "eye",
)


def nt(left, right, precision=None):
    return lax.dot_general(
        left, right, (((1,), (1,)), ((), ())),
        preferred_element_type=F32, precision=precision,
    )


def nn(left, right, precision=None):
    return jnp.dot(left, right, preferred_element_type=F32, precision=precision)


def contract_kernel(
    phi, near, partner, far, near_freq, partner_freq, far_freq, near_col, slot_row, live,
    spread_b, spread_a, both_two, both_three, mask_two, mask_three, first, second,
    first_rows, eye, rates, by_slot, y_all, z_all, w_first, w_second, w_third, near_acc,
):
    slots = near.shape[0]
    for group in range(GROUPS):
        force = phi[pl.ds(group * WIDE, WIDE), :]

        def fill(t, carry):
            y_all[t, group] = nt(far[t], force).astype(BF16)
            return carry

        lax.fori_loop(0, slots, fill, 0, unroll=4)
    w_first[...] = nn(near_freq[...], first[...])
    w_second[...] = nn(partner_freq[...], second[...])
    third = nt(eye[...], far_freq[...])
    for t in range(slots):
        w_third[t] = jnp.broadcast_to(third[:, t : t + 1], (ROWS, WIDE))
    lane = lax.broadcasted_iota(jnp.int32, (2 * ROWS, 128), 1)
    column = lax.broadcasted_iota(jnp.int32, (1, 128), 1)
    wide_lane = lax.broadcasted_iota(jnp.int32, (1, WIDE), 1) % 128
    block = wide_lane % 40
    used = (block < NB) & (wide_lane < 120)

    def one(t, far_cols):
        spread = nt(spread_b[...], partner[t]).astype(BF16)
        two = (nn(spread, both_two[...]) * jnp.concatenate([mask_two[...]] * 2, 1)).astype(BF16)
        spread = nt(spread_a[...], near[t]).astype(BF16)
        three = (nn(spread, both_three[...]) * jnp.concatenate([mask_three[...]] * 2, 1)).astype(BF16)
        for group in range(GROUPS):
            part = nn(y_all[t, group], two)
            real = part[:ROWS, :WIDE] - part[ROWS:, WIDE:]
            imag = part[:ROWS, WIDE:] + part[ROWS:, :WIDE]
            z_all[group] = jnp.concatenate([real, imag], 0)
        w1 = w_first[pl.ds(t, 1), :]
        w3 = w_third[t]
        inv_third = jnp.where(w3 > 0, 1.0 / w3, 0.0)
        total = jnp.zeros((ROWS, WIDE), F32)
        for group in range(GROUPS):
            half, place = divmod(group, 3)
            tiles = []
            for out_half in range(2):
                pieces = []
                for out_place in range(3):
                    piece = z_all[3 * out_half + out_place, :, pl.ds(128 * half, 128)]
                    shift = (40 * (out_place - place)) % 128
                    pieces.append(pltpu.roll(piece, shift, 1) if shift else piece)
                tiles.append(
                    jnp.where(
                        lane < 40,
                        pieces[0],
                        jnp.where(lane < 80, pieces[1], jnp.where(lane < 120, pieces[2], 0.0)),
                    )
                )
            part = nn(jnp.concatenate(tiles, 1).astype(BF16), three)
            real = part[:ROWS, :WIDE] - part[ROWS:, WIDE:]
            imag = part[:ROWS, WIDE:] + part[ROWS:, :WIDE]
            power = real * real + imag * imag
            w2 = w_second[pl.ds(t, 1), pl.ds(group * WIDE, WIDE)]
            offset = ((w1 + w2) - w3) * (1.0 / smear_width)
            inverse = jnp.where(used, 1.0 / jnp.where(used, w1 * w2 * NB, 1.0), 0.0)
            total = total + power * jnp.exp(-offset * offset) * inverse
        total = total * inv_third
        alive = (t < live[0]).astype(F32)
        near_acc[pl.ds(t, 1), :] = jnp.sum(total, axis=0, keepdims=True) * alive
        sums = jnp.sum(total, axis=1, keepdims=True) * alive
        return far_cols + jnp.where(column == t, sums, 0.0)

    far_cols = lax.fori_loop(0, slots, one, jnp.zeros((ROWS, 128), F32))
    near_cols = nt(first_rows[...], near_acc[...], EXACT)
    q_count = rates.shape[1]
    to_q = (
        lax.broadcasted_iota(jnp.int32, (slots, q_count), 1) == near_col[...]
    ).astype(F32)
    rates[...] = nn(near_cols, to_q, EXACT)[:NB]
    to_slot = (
        lax.broadcasted_iota(jnp.int32, (by_slot.shape[0], slots), 0) == slot_row[...]
    ).astype(F32)
    by_slot[...] = nt(to_slot, far_cols[:, :slots], EXACT)[:, :NB]


def finish_kernel(rates, returned, rows, out):
    slots, q_count = returned.shape[0], rates.shape[1]
    eye = (
        lax.broadcasted_iota(jnp.int32, (ROWS, NB), 0)
        == lax.broadcasted_iota(jnp.int32, (ROWS, NB), 1)
    ).astype(F32)
    back = nt(eye, returned[...], EXACT)
    to_q = (lax.broadcasted_iota(jnp.int32, (slots, q_count), 1) == rows[...]).astype(F32)
    out[...] = rates[...] + nn(back, to_q, EXACT)[:NB]


def as_rows(vecs):
    count = vecs.shape[0]
    parts = vecs.reshape(count, 2, NB, NB)
    return jnp.pad(parts, ((0, 0), (0, 0), (0, ROWS - NB), (0, 0))).reshape(count, 2 * ROWS, NB)


def take(array, rows):
    return array.at[rows].get(mode="promise_in_bounds")


def on_device(eigvec, omega, phi, send_rows, local_q, partner_q, slot_ref, tri_count):
    owned = eigvec.shape[0]
    outgoing = send_rows[0]
    slots = local_q.shape[0]
    sent = jnp.concatenate([take(eigvec, outgoing), take(omega, outgoing)], 1)
    arrived = lax.all_to_all(sent, "pb", split_axis=0, concat_axis=0, tiled=True)
    force = jnp.pad(
        jnp.pad(phi, ((0, 0), (0, ROWS - NB), (0, 0))).reshape(2 * GROUPS, 3 * ROWS, NB),
        ((0, 0), (0, 8), (0, 0)),
    ).reshape(GROUPS * WIDE, NB)
    far_pair = take(arrived, slot_ref)
    far = as_rows(far_pair[:, : 2 * NB * NB])
    sign = jnp.where(jnp.arange(2 * ROWS) < ROWS, 1, -1).astype(BF16)
    far = far * sign[None, :, None]
    held = tables()
    vmem = pl.BlockSpec(memory_space=pltpu.VMEM)
    rates, by_slot = pl.pallas_call(
        contract_kernel,
        out_shape=(
            jax.ShapeDtypeStruct((NB, owned), F32),
            jax.ShapeDtypeStruct((outgoing.shape[0], NB), F32),
        ),
        in_specs=[vmem] * 9 + [pl.BlockSpec(memory_space=pltpu.SMEM)] + [vmem] * len(NAMES),
        out_specs=(vmem, vmem),
        scratch_shapes=[
            pltpu.VMEM((slots, GROUPS, 2 * ROWS, WIDE), BF16),
            pltpu.VMEM((GROUPS, 2 * ROWS, WIDE), F32),
            pltpu.VMEM((slots, WIDE), F32),
            pltpu.VMEM((slots, GROUPS * WIDE), F32),
            pltpu.VMEM((slots, ROWS, WIDE), F32),
            pltpu.VMEM((slots, WIDE), F32),
        ],
        compiler_params=pltpu.CompilerParams(vmem_limit_bytes=48 * 2**20),
    )(
        force,
        as_rows(take(eigvec, local_q)),
        as_rows(take(eigvec, partner_q)),
        far,
        take(omega, local_q),
        take(omega, partner_q),
        far_pair[:, 2 * NB * NB :],
        local_q[:, None],
        slot_ref[None, :],
        tri_count,
        *[jnp.asarray(held[name]) for name in NAMES],
    )
    returned = lax.all_to_all(by_slot, "pb", split_axis=0, concat_axis=0, tiled=True)
    return pl.pallas_call(
        finish_kernel,
        out_shape=jax.ShapeDtypeStruct((NB, owned), F32),
        in_specs=[vmem] * 3,
        out_specs=vmem,
    )(rates, returned, outgoing[:, None])


def solution(mesh):
    split = P(("groups", "pb"))
    rows = P(("groups", "pb"), None)
    return jax.shard_map(
        on_device,
        mesh=mesh,
        in_specs=(rows, rows, P(), rows, split, split, split, split),
        out_specs=P(None, ("groups", "pb")),
        check_vma=False,
    )
```

time: 157 us -> 63.9 us (0.41)
  matrix products: 79.3 us -> 0 us
  Pallas kernels: 0 us -> 29.4 us
  local copies, waits for them, and re-layouts: 33.6 us -> 11.5 us
  other arithmetic: 11.7 us -> 0.88 us
  starting transfers between devices: 16.9 us -> 10.9 us
  waiting for transfers between devices: 13.5 us -> 9.79 us
    dot_general x10 -> x0, matrix products: 79.3 us -> none  [the longest x1 17.6 us: triplet_rates(): jnp.einsum('tva,tamn->tvmn', near_imag, z_real, preferred_element_type=jn...]
    pallas_call x0 -> x2, Pallas kernels: none -> 29.4 us  [the longest x1 27.6 us: on_device(): pl.pallas_call(contract_kernel, out_shape=(jax.ShapeDtypeStruct((NB, owne...]
    convert_element_type x2 -> x0, local copies, waits for them, and re-layouts: 19.7 us -> none  [the longest x1 9.87 us: triplet_rates(): z_imag = z_imag.astype(jnp.bfloat16)]
    all_to_all x3 -> x2, starting transfers between devices: 16.9 us -> 10.9 us  [the longest x1 7.41 us: on_device(): lax.all_to_all(sent, 'pb', split_axis=0, concat_axis=0, tiled=True)]
    select_n x9 -> x4, other arithmetic: 4.47 us -> 0.67 us  [take(): return array.at[rows].get(mode='promise_in_bounds')]
    all_to_all x3 -> x2, waiting for transfers between devices: 13.5 us -> 9.79 us  [the longest x1 5.77 us: on_device(): lax.all_to_all(by_slot, 'pb', split_axis=0, concat_axis=0, tiled=True)]
    scatter-add x3 -> x0, other arithmetic: 3.03 us -> none  [the longest x1 1.37 us: on_device(): by_slot = by_slot.at[:, slot_ref].add(far_terms.T)]
    while x8 -> x0, local copies, waits for them, and re-layouts: 2.52 us -> none
  transfers between devices with their start and end apart: 3 -> 2, of which waited for: 2 -> 2; matrix products, arithmetic and copies ran while one was open for 7% -> 7% of each run, Pallas kernels for 0% -> 0%
where the time goes in v1:
time: 63.9 us; the launch traced here: 63.5 us
  Pallas kernels  29.4 us (46%)
  local copies, waits for them, and re-layouts  11.5 us (18%)
  starting transfers between devices  10.9 us (17%)
  waiting for transfers between devices  9.79 us (15%)
  between operations  1.04 us (2%)
  other arithmetic  0.88 us (1%)
    pallas_call x1, Pallas kernels, on_device(): pl.pallas_call(contract_kernel, out_shape=(jax.ShapeDtypeStruct((NB, owne...  27.6 us
    all_to_all x1, starting transfers between devices, on_device(): lax.all_to_all(sent, 'pb', split_axis=0, concat_axis=0, tiled=True)  7.41 us
    all_to_all x1, waiting for transfers between devices, on_device(): lax.all_to_all(by_slot, 'pb', split_axis=0, concat_axis=0, tiled=True)  5.77 us
    gather x7, local copies, waits for them, and re-layouts, take(): return array.at[rows].get(mode='promise_in_bounds')  4.26 us
    all_to_all x1, waiting for transfers between devices, on_device(): lax.all_to_all(sent, 'pb', split_axis=0, concat_axis=0, tiled=True)  4.02 us
    unnamed x36, local copies, waits for them, and re-layouts  3.94 us
    all_to_all x1, starting transfers between devices, on_device(): lax.all_to_all(by_slot, 'pb', split_axis=0, concat_axis=0, tiled=True)  3.49 us
    pallas_call x1, Pallas kernels, on_device(): pl.pallas_call(finish_kernel, out_shape=jax.ShapeDtypeStruct((NB, owned),...  1.77 us
  transfers between devices with their start and end apart: 2, of which 2 were waited for; matrix products, arithmetic and copies ran while one was open for 7% of the time, Pallas kernels for 0%

profile of v1, /device:TPU:0, one launch (start us, length us, event | category | flops | bytes accessed | tf_op | source)
XLA Modules:
  0.0 63.5 jit_solution(8772181909854161018)
XLA Ops:
  0.0 0.7 %fusion.1 = s32[32]{0:T(128)S(1)} fusion(s32[1,32]{1,0:T(1,128)} %param.21), kind=kLoop, calls=%fused_computation.19 | loop fusion | flops 96 | bytes 256 | tf_op jit(solution)/shard_map/select_n | solution.py:191
  0.7 0.9 %copy.30 = bf16[256,36]{1,0:T(8,128)(2,1)S(1)} copy(bf16[256,36]{0,1:T(8,128)(2,1)} %param.19) | data formatting | bytes 36864 | tf_op args[1]
  1.5 1.8 %copy.27 = bf16[256,2592]{1,0:T(8,128)(2,1)S(1)} copy(bf16[256,2592]{0,1:T(8,128)(2,1)} %param.18) | data formatting | bytes 2654208 | tf_op args[0]
  3.3 0.0 copy-start.16
  3.3 0.6 gather_fusion.3
  3.9 0.0 copy-start.14
  3.9 0.7 %gather_fusion.2 = bf16[32,2592]{1,0:T(8,128)(2,1)S(1)} fusion(bf16[256,2592]{1,0:T(8,128)(2,1)S(1)} %copy.27, s32[1024]{0:T(1024)S(1)} %pad_clamp_fusion.1), kind=kCustom, calls=%fused_computation.2 | custom fusion | bytes 331904 | tf_op jit(solution)/shard_map/gather | solution.py:191
  4.6 0.0 copy-start.12
  4.6 0.1 pad_maximum_fusion
  4.7 0.7 %all_to_all.15 = bf16[16,2,2628]{2,1,0:T(2,128)(2,1)} reshape(bf16[32,2628]{1,0:T(8,128)(2,1)S(1)} %pad_maximum_fusion) | data formatting | bytes 336384 | tf_op jit(solution)/shard_map/all_to_all | solution.py:199
  5.4 7.4 %all-to-all-start = ((bf16[16,2,2628]{2,1,0:T(2,128)(2,1)}), bf16[16,2,2628]{2,1,0:T(2,128)(2,1)S(1)}, u32[]{:S(2)}, u32[]{:S(2)}) async-start(bf16[16,2,2628]{2,1,0:T(2,128)(2,1)} %all_to_all.15), calls=%async_computation | async-start | bytes 344064 | tf_op jit(solution)/shard_map/all_to_all | solution.py:199
  12.9 0.0 copy-done.16
  12.9 0.6 gather_fusion.6
  13.5 0.6 gather_fusion.1
  14.1 0.0 copy-done.14
  14.1 0.6 gather_fusion.5
  14.7 0.6 gather_fusion
  16.0 0.1 copy.33.near_col
  16.1 0.0 copy-done.12
  16.1 0.1 pad.18
  16.1 0.0 copy-start.11
  16.1 0.1 pad.19
  16.3 0.4 reshape.64
  16.7 0.1 pad.20
  16.7 0.4 reshape.66
  17.2 0.1 pad.21
  17.2 0.0 copy-done.11
  17.3 0.0 copy-start
  17.3 0.0 copy-start.1
  17.3 0.0 copy-start.2
  17.3 0.0 copy-start.3
  17.3 0.0 copy-start.4
  17.3 0.0 copy-start.5
  17.3 0.0 copy-start.6
  17.4 0.0 copy-start.8
  17.4 0.0 copy-start.9
  17.4 0.0 copy-start.10
  17.4 4.0 %all-to-all-done = bf16[16,2,2628]{2,1,0:T(2,128)(2,1)S(1)} async-done(((bf16[16,2,2628]{2,1,0:T(2,128)(2,1)}), bf16[16,2,2628]{2,1,0:T(2,128)(2,1)S(1)}, u32[]{:S(2)}, u32[]{:S(2)}) %all-to-all-start) | async-done | bytes 168224 | tf_op jit(solution)/shard_map/all_to_all | solution.py:199
  21.4 0.1 all_to_all.17
  21.6 0.6 gather_fusion.4
  22.2 0.1 slice.23.far_freq
  22.2 0.4 reshape.68
  22.7 0.1 pad.22
  22.7 0.1 bitcast_multiply_fusion.far
  22.8 0.0 copy-start.15
  22.8 0.0 copy-done
  22.9 0.0 copy-done.1
  22.9 0.0 copy-done.2
  22.9 0.0 copy-done.3
  22.9 0.0 copy-done.4
  22.9 0.0 copy-done.5
  22.9 0.0 copy-done.6
  22.9 0.0 copy-done.8
  22.9 0.0 copy-done.9
  22.9 0.0 copy-done.10
  22.9 27.6 %shard_map.172 = (f32[36,256]{1,0:T(8,128)S(1)}, f32[32,36]{1,0:T(8,128)}) custom-call(bf16[1536,36]{1,0:T(8,128)(2,1)S(1)} %bitcast.15, bf16[16,80,36]{2,1,0:T(8,128)(2,1)S(1)} %bitcast.16, bf16[16,80,36]{2,1,0:T(8,128)(2,1)S(1)} %bitcast.17, bf16[16,80,36]{2,1,0:T(8,128)(2,1)S(1)} %bitcast_multiply_fusion.far, bf16[16,36]{1,0:T(8,128)(2,1)S(1)} %gather_fusion.5, ...), custom_call_target="tpu_custom_call" | custom-call | tf_op jit(solution)/shard_map/pallas_call | solution.py:210
  50.6 0.0 copy-start.7
  50.6 0.6 copy-done.7
  51.2 3.5 %all-to-all-start.1 = ((f32[16,2,36]{2,1,0:T(2,128)}), f32[16,2,36]{2,1,0:T(2,128)S(1)}, u32[]{:S(2)}, u32[]{:S(2)}) async-start(f32[16,2,36]{2,1,0:T(2,128)} %bitcast.9), calls=%async_computation.1 | async-start | bytes 32768 | tf_op jit(solution)/shard_map/all_to_all | solution.py:240
  54.7 0.0 copy-done.15
  54.7 0.7 %copy.34.rows = s32[32,1]{1,0:T(8,128)} copy(s32[32,1]{0,1:T(1,128)S(1)} %bitcast.23) | data formatting | bytes 256 | tf_op jit(solution)/shard_map/squeeze | solution.py:196
  55.4 5.8 %all-to-all-done.1 = f32[16,2,36]{2,1,0:T(2,128)S(1)} async-done(((f32[16,2,36]{2,1,0:T(2,128)}), f32[16,2,36]{2,1,0:T(2,128)S(1)}, u32[]{:S(2)}, u32[]{:S(2)}) %all-to-all-start.1) | async-done | bytes 4640 | tf_op jit(solution)/shard_map/all_to_all | solution.py:240
  61.2 0.6 copy-done.13
  61.7 1.8 %shard_map.173 = f32[36,256]{1,0:T(8,128)} custom-call(f32[36,256]{1,0:T(8,128)} %copy-done.7, f32[32,36]{1,0:T(8,128)} %bitcast.21, s32[32,1]{1,0:T(8,128)} %copy.34.rows), custom_call_target="tpu_custom_call" | custom-call | tf_op jit(solution)/shard_map/pallas_call | solution.py:241
  (9 shorter events, 0.0 us)
Async XLA Ops:
  3.3 9.6 %copy-start.16 = (s32[16]{0:T(128)S(1)}, s32[16]{0:T(128)}, u32[]{:S(2)}) copy-start(s32[16]{0:T(128)} %param.23) | copy-start | bytes 196
  3.9 10.2 %copy-start.14 = (s32[16]{0:T(128)S(1)}, s32[16]{0:T(128)}, u32[]{:S(2)}) copy-start(s32[16]{0:T(128)} %param.22) | copy-start | bytes 196
  4.6 11.4 %copy-start.12 = (bf16[36,36,36]{2,1,0:T(8,128)(2,1)S(1)}, bf16[36,36,36]{2,1,0:T(8,128)(2,1)}, u32[]{:S(2)}) copy-start(bf16[36,36,36]{2,1,0:T(8,128)(2,1)} %param.20) | copy-start | bytes 279940
  5.4 16.0 %all-to-all-start = ((bf16[16,2,2628]{2,1,0:T(2,128)(2,1)}), bf16[16,2,2628]{2,1,0:T(2,128)(2,1)S(1)}, u32[]{:S(2)}, u32[]{:S(2)}) async-start(bf16[16,2,2628]{2,1,0:T(2,128)(2,1)} %all_to_all.15), calls=%async_computation | async-start | bytes 344064 | tf_op jit(solution)/shard_map/all_to_all | solution.py:199
  16.1 1.1 %copy-start.11 = (s32[16]{0:T(128)S(1)}, s32[16]{0:T(128)}, u32[]{:S(2)}) copy-start(s32[16]{0:T(128)} %param.24) | copy-start | bytes 196
  17.3 5.6 %copy-start = (f32[256,256]{1,0:T(8,128)S(1)}, f32[256,256]{1,0:T(8,128)}, u32[]{:S(2)}) copy-start(f32[256,256]{1,0:T(8,128)} %constant.42.clone.mask_three) | copy-start | bytes 786436
  17.3 5.6 %copy-start.1 = (f32[256,256]{1,0:T(8,128)S(1)}, f32[256,256]{1,0:T(8,128)}, u32[]{:S(2)}) copy-start(f32[256,256]{1,0:T(8,128)} %constant.41.clone.mask_two) | copy-start | bytes 786436
  17.3 5.6 %copy-start.2 = (bf16[36,1536]{1,0:T(8,128)(2,1)S(1)}, bf16[36,1536]{1,0:T(8,128)(2,1)}, u32[]{:S(2)}) copy-start(bf16[36,1536]{1,0:T(8,128)(2,1)} %constant.44.clone.second) | copy-start | bytes 331780
  17.3 5.6 %copy-start.3 = (bf16[80,512]{1,0:T(8,128)(2,1)S(1)}, bf16[80,512]{1,0:T(8,128)(2,1)}, u32[]{:S(2)}) copy-start(bf16[80,512]{1,0:T(8,128)(2,1)} %constant.40.clone.both_three) | copy-start | bytes 245764
  17.3 5.6 %copy-start.4 = (bf16[80,512]{1,0:T(8,128)(2,1)S(1)}, bf16[80,512]{1,0:T(8,128)(2,1)}, u32[]{:S(2)}) copy-start(bf16[80,512]{1,0:T(8,128)(2,1)} %constant.39.clone.both_two) | copy-start | bytes 245764
  17.3 5.6 %copy-start.5 = (bf16[256,36]{1,0:T(8,128)(2,1)S(1)}, bf16[256,36]{1,0:T(8,128)(2,1)}, u32[]{:S(2)}) copy-start(bf16[256,36]{1,0:T(8,128)(2,1)} %constant.38.clone.spread_a) | copy-start | bytes 55300
  17.3 5.6 %copy-start.6 = (bf16[256,36]{1,0:T(8,128)(2,1)S(1)}, bf16[256,36]{1,0:T(8,128)(2,1)}, u32[]{:S(2)}) copy-start(bf16[256,36]{1,0:T(8,128)(2,1)} %constant.16.clone.spread_b) | copy-start | bytes 55300
  17.4 5.6 %copy-start.8 = (f32[40,256]{1,0:T(8,128)S(1)}, f32[40,256]{1,0:T(8,128)}, u32[]{:S(2)}) copy-start(f32[40,256]{1,0:T(8,128)} %constant.45.clone.first_rows) | copy-start | bytes 122884
  17.4 5.6 %copy-start.9 = (bf16[36,256]{1,0:T(8,128)(2,1)S(1)}, bf16[36,256]{1,0:T(8,128)(2,1)}, u32[]{:S(2)}) copy-start(bf16[36,256]{1,0:T(8,128)(2,1)} %constant.43.clone.first) | copy-start | bytes 55300
  17.4 5.6 %copy-start.10 = (bf16[40,36]{1,0:T(8,128)(2,1)S(1)}, bf16[40,36]{1,0:T(8,128)(2,1)}, u32[]{:S(2)}) copy-start(bf16[40,36]{1,0:T(8,128)(2,1)} %constant.46.clone.eye) | copy-start | bytes 8644
  22.8 31.9 %copy-start.15 = (s32[1,32]{1,0:T(1,128)S(1)}, s32[1,32]{1,0:T(1,128)}, u32[]{:S(2)}) copy-start(s32[1,32]{1,0:T(1,128)} %param.21) | copy-start | bytes 388
  50.6 0.6 copy-start.7
  51.2 10.0 %all-to-all-start.1 = ((f32[16,2,36]{2,1,0:T(2,128)}), f32[16,2,36]{2,1,0:T(2,128)S(1)}, u32[]{:S(2)}, u32[]{:S(2)}) async-start(f32[16,2,36]{2,1,0:T(2,128)} %bitcast.9), calls=%async_computation.1 | async-start | bytes 32768 | tf_op jit(solution)/shard_map/all_to_all | solution.py:240
  61.1 0.6 copy-start.13

commit v2 on v1

--- a/solution.py
+++ b/solution.py
@@ -47,33 +47,29 @@
         for at in range(WIDE):
             if inner[at] >= 0:
                 second[group, group * GROUPS + inner[at], at] = 1
-    both_two = np.zeros((2 * ROWS, 2 * WIDE), np.float32)
-    both_two[:ROWS, :WIDE] = pick
-    both_two[ROWS:, WIDE:] = pick
-    both_three = np.zeros((2 * ROWS, 2 * WIDE), np.float32)
-    both_three[:NB, :WIDE] = by_first
-    both_three[ROWS : ROWS + NB, WIDE:] = by_first
+    lift_b = np.zeros((2, WIDE, 128), np.float32)
+    lift_a = np.zeros((2, WIDE, 128), np.float32)
+    for part in range(2):
+        lift_b[part, :, part * NB : (part + 1) * NB] = spread_b
+        lift_a[part, :, part * NB : (part + 1) * NB] = spread_a
     by_first_rows = np.zeros((ROWS, WIDE), np.float32)
     by_first_rows[:NB] = by_first
-    eye = np.zeros((ROWS, NB), np.float32)
-    eye[:NB] = np.eye(NB)
     return dict(
-        spread_b=spread_b.astype(BF16),
-        spread_a=spread_a.astype(BF16),
-        both_two=both_two.astype(BF16),
-        both_three=both_three.astype(BF16),
-        mask_two=mask_two,
-        mask_three=mask_three,
+        spread_b=lift_b.astype(BF16),
+        spread_a=lift_a.astype(BF16),
+        both_two=pick.astype(BF16),
+        both_three=by_first_rows.astype(BF16),
+        mask_two=mask_two.astype(BF16),
+        mask_three=mask_three.astype(BF16),
         first=by_first.astype(BF16),
         second=np.transpose(second, (1, 0, 2)).reshape(NB, GROUPS * WIDE).astype(BF16),
         first_rows=by_first_rows,
-        eye=eye.astype(BF16),
     )
 
 
 NAMES = (
     "spread_b", "spread_a", "both_two", "both_three", "mask_two",
-    "mask_three", "first", "second", "first_rows", "eye",
+    "mask_three", "first", "second", "first_rows",
 )
 
 
@@ -88,36 +84,112 @@
     return jnp.dot(left, right, preferred_element_type=F32, precision=precision)
 
 
+def peers(count):
+    me = lax.axis_index("pb")
+
+    def at(step):
+        return lax.rem(me + step, count)
+
+    return me, at
+
+
+def greet(count):
+    _, at = peers(count)
+    barrier = pltpu.get_barrier_semaphore()
+
+    def signal(step, carry):
+        pl.semaphore_signal(
+            barrier, inc=1, device_id={"pb": at(step)}, device_id_type=pl.DeviceIdType.MESH
+        )
+        return carry
+
+    lax.fori_loop(1, count, signal, 0)
+    pl.semaphore_wait(barrier, count - 1)
+
+
+def exchange(count, source, target, send_sem, recv_sem):
+    me, at = peers(count)
+
+    def copy(peer, slot):
+        return pltpu.make_async_remote_copy(
+            src_ref=source.at[peer],
+            dst_ref=target.at[slot],
+            send_sem=send_sem.at[peer],
+            recv_sem=recv_sem.at[slot],
+            device_id={"pb": peer},
+            device_id_type=pl.DeviceIdType.MESH,
+        )
+
+    def start(step, carry):
+        copy(at(step), me).start()
+        return carry
+
+    def finish(step, carry):
+        copy(at(step), at(step)).wait_recv()
+        return carry
+
+    def drain(step, carry):
+        copy(at(step), me).wait_send()
+        return carry
+
+    return (
+        lambda: lax.fori_loop(1, count, start, 0),
+        lambda: lax.fori_loop(1, count, finish, 0),
+        lambda: lax.fori_loop(1, count, drain, 0),
+    )
+
+
 def contract_kernel(
-    phi, near, partner, far, near_freq, partner_freq, far_freq, near_col, slot_row, live,
-    spread_b, spread_a, both_two, both_three, mask_two, mask_three, first, second,
-    first_rows, eye, rates, by_slot, y_all, z_all, w_first, w_second, w_third, near_acc,
+    count, cap, slot_ref, live, outgoing, near, partner, force, near_freq, partner_freq,
+    near_col, slot_row, spread_b, spread_a, both_two, both_three, mask_two, mask_three,
+    first, second, first_rows, rates, by_slot, arrived, two_all, three_all, y_all, z_all,
+    w_first, w_second, w_third, near_acc, send_sem, recv_sem,
 ):
     slots = near.shape[0]
-    for group in range(GROUPS):
-        force = phi[pl.ds(group * WIDE, WIDE), :]
-
-        def fill(t, carry):
-            y_all[t, group] = nt(far[t], force).astype(BF16)
-            return carry
-
-        lax.fori_loop(0, slots, fill, 0, unroll=4)
+    me, _ = peers(count)
+    start, finish, drain = exchange(count, outgoing, arrived, send_sem, recv_sem)
+    greet(count)
+    start()
+    arrived[me] = outgoing[me]
+
     w_first[...] = nn(near_freq[...], first[...])
     w_second[...] = nn(partner_freq[...], second[...])
-    third = nt(eye[...], far_freq[...])
-    for t in range(slots):
-        w_third[t] = jnp.broadcast_to(third[:, t : t + 1], (ROWS, WIDE))
+
+    def prepare(t, carry):
+        for own, spread, picks, mask, held in (
+            (partner, spread_b, both_two, mask_two, two_all),
+            (near, spread_a, both_three, mask_three, three_all),
+        ):
+            vecs = own[t]
+            for part in range(2):
+                lifted = nt(spread[part], vecs).astype(BF16)
+                held[t, :, pl.ds(part * WIDE, WIDE)] = (
+                    nn(lifted, picks[...]).astype(BF16) * mask[...]
+                )
+        return carry
+
+    lax.fori_loop(0, slots, prepare, 0, unroll=2)
+    finish()
+
+    def fill(t, carry):
+        far = arrived[slot_ref[t] // cap, slot_ref[t] % cap]
+        w_third[t] = jnp.broadcast_to(far[:, 2 * NB : 2 * NB + 1].astype(F32), (ROWS, WIDE))
+        for group in range(GROUPS):
+            for part in range(2):
+                rows = pl.ds(part * ROWS, ROWS)
+                tile = force[part, pl.ds(group * WIDE, WIDE), :]
+                y_all[t, group, rows] = nt(far, tile).astype(BF16)
+        return carry
+
+    lax.fori_loop(0, slots, fill, 0, unroll=2)
     lane = lax.broadcasted_iota(jnp.int32, (2 * ROWS, 128), 1)
     column = lax.broadcasted_iota(jnp.int32, (1, 128), 1)
     wide_lane = lax.broadcasted_iota(jnp.int32, (1, WIDE), 1) % 128
-    block = wide_lane % 40
-    used = (block < NB) & (wide_lane < 120)
+    used = (wide_lane % 40 < NB) & (wide_lane < 120)
 
     def one(t, far_cols):
-        spread = nt(spread_b[...], partner[t]).astype(BF16)
-        two = (nn(spread, both_two[...]) * jnp.concatenate([mask_two[...]] * 2, 1)).astype(BF16)
-        spread = nt(spread_a[...], near[t]).astype(BF16)
-        three = (nn(spread, both_three[...]) * jnp.concatenate([mask_three[...]] * 2, 1)).astype(BF16)
+        two = two_all[t]
+        three = three_all[t]
         for group in range(GROUPS):
             part = nn(y_all[t, group], two)
             real = part[:ROWS, :WIDE] - part[ROWS:, WIDE:]
@@ -165,26 +237,30 @@
     ).astype(F32)
     rates[...] = nn(near_cols, to_q, EXACT)[:NB]
     to_slot = (
-        lax.broadcasted_iota(jnp.int32, (by_slot.shape[0], slots), 0) == slot_row[...]
+        lax.broadcasted_iota(jnp.int32, (count * cap, slots), 0) == slot_row[...]
     ).astype(F32)
-    by_slot[...] = nt(to_slot, far_cols[:, :slots], EXACT)[:, :NB]
-
-
-def finish_kernel(rates, returned, rows, out):
-    slots, q_count = returned.shape[0], rates.shape[1]
+    sums = nt(to_slot, far_cols[:, :slots], EXACT)[:, :NB]
+    for owner in range(count):
+        by_slot[owner] = sums[owner * cap : (owner + 1) * cap]
+    drain()
+
+
+def finish_kernel(count, rates, sent, rows, out, returned, send_sem, recv_sem):
+    me, _ = peers(count)
+    start, finish, drain = exchange(count, sent, returned, send_sem, recv_sem)
+    greet(count)
+    start()
+    returned[me] = sent[me]
+    slots, q_count = rows.shape[0], rates.shape[1]
     eye = (
         lax.broadcasted_iota(jnp.int32, (ROWS, NB), 0)
         == lax.broadcasted_iota(jnp.int32, (ROWS, NB), 1)
     ).astype(F32)
-    back = nt(eye, returned[...], EXACT)
     to_q = (lax.broadcasted_iota(jnp.int32, (slots, q_count), 1) == rows[...]).astype(F32)
+    finish()
+    back = nt(eye, jnp.concatenate([returned[owner] for owner in range(count)], 0), EXACT)
     out[...] = rates[...] + nn(back, to_q, EXACT)[:NB]
-
-
-def as_rows(vecs):
-    count = vecs.shape[0]
-    parts = vecs.reshape(count, 2, NB, NB)
-    return jnp.pad(parts, ((0, 0), (0, 0), (0, ROWS - NB), (0, 0))).reshape(count, 2 * ROWS, NB)
+    drain()
 
 
 def take(array, rows):
@@ -195,55 +271,76 @@
     owned = eigvec.shape[0]
     outgoing = send_rows[0]
     slots = local_q.shape[0]
-    sent = jnp.concatenate([take(eigvec, outgoing), take(omega, outgoing)], 1)
-    arrived = lax.all_to_all(sent, "pb", split_axis=0, concat_axis=0, tiled=True)
-    force = jnp.pad(
+    count = lax.axis_size("pb")
+    cap = outgoing.shape[0] // count
+    sent = outgoing.shape[0]
+    wanted = jnp.concatenate([outgoing, local_q, partner_q])
+    vecs = take(eigvec, wanted).reshape(-1, 2, NB, NB)
+    freqs = take(omega, wanted)
+    packed = jnp.concatenate([vecs[:, 0], vecs[:, 1], freqs[:, :, None]], 2)
+    packed = jnp.pad(packed, ((0, 0), (0, ROWS - NB), (0, 127 - 2 * NB)))
+    tiles = jnp.pad(
         jnp.pad(phi, ((0, 0), (0, ROWS - NB), (0, 0))).reshape(2 * GROUPS, 3 * ROWS, NB),
         ((0, 0), (0, 8), (0, 0)),
     ).reshape(GROUPS * WIDE, NB)
-    far_pair = take(arrived, slot_ref)
-    far = as_rows(far_pair[:, : 2 * NB * NB])
-    sign = jnp.where(jnp.arange(2 * ROWS) < ROWS, 1, -1).astype(BF16)
-    far = far * sign[None, :, None]
+    force = jnp.stack(
+        [
+            jnp.pad(tiles, ((0, 0), (0, 128 - NB))),
+            jnp.pad(-tiles, ((0, 0), (NB, 128 - 2 * NB))),
+        ]
+    )
     held = tables()
     vmem = pl.BlockSpec(memory_space=pltpu.VMEM)
+    smem = pl.BlockSpec(memory_space=pltpu.SMEM)
     rates, by_slot = pl.pallas_call(
-        contract_kernel,
+        functools.partial(contract_kernel, count, cap),
         out_shape=(
             jax.ShapeDtypeStruct((NB, owned), F32),
-            jax.ShapeDtypeStruct((outgoing.shape[0], NB), F32),
+            jax.ShapeDtypeStruct((count, cap, NB), F32),
         ),
-        in_specs=[vmem] * 9 + [pl.BlockSpec(memory_space=pltpu.SMEM)] + [vmem] * len(NAMES),
+        in_specs=[smem] * 2 + [vmem] * (8 + len(NAMES)),
         out_specs=(vmem, vmem),
         scratch_shapes=[
+            pltpu.VMEM((count, cap, ROWS, 128), BF16),
+            pltpu.VMEM((slots, WIDE, 2 * WIDE), BF16),
+            pltpu.VMEM((slots, WIDE, 2 * WIDE), BF16),
             pltpu.VMEM((slots, GROUPS, 2 * ROWS, WIDE), BF16),
             pltpu.VMEM((GROUPS, 2 * ROWS, WIDE), F32),
             pltpu.VMEM((slots, WIDE), F32),
             pltpu.VMEM((slots, GROUPS * WIDE), F32),
             pltpu.VMEM((slots, ROWS, WIDE), F32),
             pltpu.VMEM((slots, WIDE), F32),
+            pltpu.SemaphoreType.DMA((count,)),
+            pltpu.SemaphoreType.DMA((count,)),
         ],
-        compiler_params=pltpu.CompilerParams(vmem_limit_bytes=48 * 2**20),
+        compiler_params=pltpu.CompilerParams(
+            vmem_limit_bytes=48 * 2**20, collective_id=0, has_side_effects=True
+        ),
     )(
+        slot_ref,
+        tri_count,
+        packed[:sent].reshape(count, cap, ROWS, 128),
+        packed[sent : sent + slots],
+        packed[sent + slots :],
         force,
-        as_rows(take(eigvec, local_q)),
-        as_rows(take(eigvec, partner_q)),
-        far,
-        take(omega, local_q),
-        take(omega, partner_q),
-        far_pair[:, 2 * NB * NB :],
+        freqs[sent : sent + slots],
+        freqs[sent + slots :],
         local_q[:, None],
         slot_ref[None, :],
-        tri_count,
         *[jnp.asarray(held[name]) for name in NAMES],
     )
-    returned = lax.all_to_all(by_slot, "pb", split_axis=0, concat_axis=0, tiled=True)
     return pl.pallas_call(
-        finish_kernel,
+        functools.partial(finish_kernel, count),
         out_shape=jax.ShapeDtypeStruct((NB, owned), F32),
         in_specs=[vmem] * 3,
         out_specs=vmem,
-    )(rates, returned, outgoing[:, None])
+        scratch_shapes=[
+            pltpu.VMEM((count, cap, NB), F32),
+            pltpu.SemaphoreType.DMA((count,)),
+            pltpu.SemaphoreType.DMA((count,)),
+        ],
+        compiler_params=pltpu.CompilerParams(collective_id=1, has_side_effects=True),
+    )(rates, by_slot, outgoing[:, None])
 
 
 def solution(mesh):

time: 63.9 us -> 59 us (0.923)
  Pallas kernels: 29.4 us -> 44.7 us
  starting transfers between devices: 10.9 us -> 0 us
  waiting for transfers between devices: 9.79 us -> 0 us
  other arithmetic: 0.88 us -> 1.7 us
    pallas_call x2, Pallas kernels: 29.4 us -> 44.7 us  [the longest x1 36.2 us: on_device(): pl.pallas_call(functools.partial(contract_kernel, count, cap), out_shape=...]
    all_to_all x2 -> x0, starting transfers between devices: 10.9 us -> none  [the longest x1 7.41 us: on_device(): lax.all_to_all(sent, 'pb', split_axis=0, concat_axis=0, tiled=True)]
    all_to_all x2 -> x0, waiting for transfers between devices: 9.79 us -> none  [the longest x1 5.77 us: on_device(): lax.all_to_all(by_slot, 'pb', split_axis=0, concat_axis=0, tiled=True)]
    gather x7 -> x2, local copies, waits for them, and re-layouts: 4.26 us -> 1.42 us  [take(): return array.at[rows].get(mode='promise_in_bounds')]
    unnamed x36 -> x35, local copies, waits for them, and re-layouts: 3.94 us -> 6.31 us
    all_to_all x2 -> x0, local copies, waits for them, and re-layouts: 0.86 us -> none  [on_device(): lax.all_to_all(sent, 'pb', split_axis=0, concat_axis=0, tiled=True)]
    concatenate x0 -> x2, local copies, waits for them, and re-layouts: none -> 0.76 us  [on_device(): wanted = jnp.concatenate([outgoing, local_q, partner_q])]
    concatenate x1, other arithmetic: 0.08 us -> 0.78 us  [on_device(): packed = jnp.concatenate([vecs[:, 0], vecs[:, 1], freqs[:, :, None]], 2)]
  transfers between devices with their start and end apart: 2 -> 0, of which waited for: 2 -> 0; matrix products, arithmetic and copies ran while one was open for 7% -> 0% of each run, Pallas kernels for 0% -> 0%
where the time goes in v2:
time: 59 us; the launch traced here: 58.6 us
  Pallas kernels  44.7 us (76%)
  local copies, waits for them, and re-layouts  11.2 us (19%)
  other arithmetic  1.7 us (3%)
  between operations  0.96 us (2%)
    pallas_call x1, Pallas kernels, on_device(): pl.pallas_call(functools.partial(contract_kernel, count, cap), out_shape=...  36.2 us
    pallas_call x1, Pallas kernels, on_device(): pl.pallas_call(functools.partial(finish_kernel, count), out_shape=jax.Sha...  8.47 us
    unnamed x35, local copies, waits for them, and re-layouts  6.31 us
    reshape x1, local copies, waits for them, and re-layouts, on_device(): vecs = take(eigvec, wanted).reshape(-1, 2, NB, NB)  1.64 us
    gather x2, local copies, waits for them, and re-layouts, take(): return array.at[rows].get(mode='promise_in_bounds')  1.42 us

profile of v2, /device:TPU:0, one launch (start us, length us, event | category | flops | bytes accessed | tf_op | source)
XLA Modules:
  0.0 58.6 jit_solution(10883134176549198419)
XLA Ops:
  0.0 0.8 %fusion.9 = s32[64]{0:T(128)S(1)} fusion(s32[16,1]{0,1:T(1,128)} %bitcast.32, s32[16,1]{0,1:T(1,128)} %bitcast.28, s32[32,1]{0,1:T(1,128)} %bitcast.30), kind=kLoop, calls=%fused_computation.20 | loop fusion | flops 320 | bytes 512 | tf_op jit(solution)/shard_map/select_n | solution.py:267
  0.8 1.8 %copy.22 = bf16[256,2592]{1,0:T(8,128)(2,1)S(1)} copy(bf16[256,2592]{0,1:T(8,128)(2,1)} %param.17) | data formatting | bytes 2654208 | tf_op args[0]
  2.6 0.8 %gather_fusion = bf16[64,2592]{1,0:T(8,128)(2,1)S(1)} fusion(bf16[256,2592]{1,0:T(8,128)(2,1)S(1)} %copy.22, s32[1024]{0:T(1024)S(1)} %pad_clamp_fusion), kind=kCustom, calls=%fused_computation | custom fusion | bytes 663808 | tf_op jit(solution)/shard_map/gather | solution.py:267
  3.4 1.6 %reshape.153 = bf16[64,2,36,36]{3,2,1,0:T(8,128)(2,1)S(1)} reshape(bf16[64,2592]{1,0:T(8,128)(2,1)S(1)} %gather_fusion) | data formatting | bytes 663552 | tf_op jit(solution)/shard_map/reshape | solution.py:278
  5.0 0.0 copy-start.13
  5.0 0.1 slice_bitcast_fusion.1
  5.1 0.6 %copy-done.13 = bf16[256,36]{0,1:T(8,128)(2,1)S(1)} copy-done((bf16[256,36]{0,1:T(8,128)(2,1)S(1)}, bf16[256,36]{0,1:T(8,128)(2,1)}, u32[]{:S(2)}) %copy-start.13) | copy-done | bytes 18456
  5.7 0.1 copy.26
  5.9 0.6 %gather_fusion.1 = bf16[64,36]{1,0:T(8,128)(2,1)S(1)} fusion(bf16[256,36]{1,0:T(8,128)(2,1)S(1)} %copy.26, s32[1024]{0:T(1024)S(1)} %pad_clamp_fusion), kind=kCustom, calls=%fused_computation.1 | custom fusion | bytes 9472 | tf_op jit(solution)/shard_map/gather | solution.py:267
  6.5 0.5 copy.28
  7.0 0.8 %fusion.8 = bf16[64,40,128]{2,1,0:T(8,128)(2,1)S(1)} fusion(bf16[64,36,1]{2,1,0:T(8,128)(2,1)S(1)} %copy.28, bf16[64,36,36]{2,1,0:T(8,128)(2,1)S(1)} %get-tuple-element.10, bf16[64,36,36]{2,1,0:T(8,128)(2,1)S(1)} %get-tuple-element.9), kind=kLoop, calls=%fused_computation.13 | loop fusion | flops 4915200 | bytes 991744 | tf_op jit(solution)/shard_map/concatenate | solution.py:280
  7.8 0.0 copy-start.12
  7.9 0.9 %copy-done.12 = bf16[36,36,36]{2,1,0:T(8,128)(2,1)S(1)} copy-done((bf16[36,36,36]{2,1,0:T(8,128)(2,1)S(1)}, bf16[36,36,36]{2,1,0:T(8,128)(2,1)}, u32[]{:S(2)}) %copy-start.12) | copy-done | bytes 93336
  8.8 0.1 pad.21
  8.9 0.1 pad.22
  9.0 0.1 bitcast_negate_fusion
  9.1 0.0 copy-start.14
  9.1 0.0 copy-start
  9.1 0.0 copy-start.1
  9.1 0.0 copy-start.2
  9.1 0.0 copy-start.3
  9.2 0.0 copy-start.4
  9.2 0.0 copy-start.6
  9.2 0.0 copy-start.7
  9.2 0.0 copy-start.8
  9.2 0.0 copy-start.9
  9.2 0.0 copy-start.11
  9.2 0.2 pad_bitcast_fusion
  9.5 0.1 pad_maximum_fusion.force
  9.5 0.0 copy-start.15
  9.6 0.2 copy-done.14
  9.8 0.1 copy.29.near_col
  10.5 0.0 copy-done
  10.5 0.0 copy-done.1
  10.5 0.0 copy-done.2
  10.5 0.0 copy-done.3
  10.5 0.0 copy-done.4
  10.5 0.0 copy-done.6
  10.5 0.0 copy-done.7
  10.6 0.0 copy-done.8
  10.6 0.0 copy-done.9
  10.6 0.0 copy-done.11
  10.6 36.2 %shard_map.163 = (f32[36,256]{1,0:T(8,128)S(1)}, f32[16,2,36]{2,1,0:T(2,128)S(1)}) custom-call(s32[16]{0:T(128)S(1)} %copy-done.11, s32[1]{0:T(128)S(6)} %copy.38.live, bf16[16,2,40,128]{3,2,1,0:T(8,128)(2,1)S(1)} %bitcast.23, bf16[16,40,128]{2,1,0:T(8,128)(2,1)S(1)} %get-tuple-element.12.near, bf16[16,40,128]{2,1,0:T(8,128)(2,1)S(1)} %get-tuple-element.11.partner, ...), custom_call_target="tpu_custom_call" | custom-call | tf_op jit(solution)/shard_map/pallas_call | solution.py:295
  46.8 0.0 copy-start.5
  46.8 0.6 %copy-done.5 = f32[36,256]{1,0:T(8,128)} copy-done((f32[36,256]{1,0:T(8,128)}, f32[36,256]{1,0:T(8,128)S(1)}, u32[]{:S(2)}) %copy-start.5) | copy-done | bytes 36888
  47.4 0.0 copy-start.10
  47.4 0.6 %copy-done.10 = f32[16,2,36]{2,1,0:T(2,128)} copy-done((f32[16,2,36]{2,1,0:T(2,128)}, f32[16,2,36]{2,1,0:T(2,128)S(1)}, u32[]{:S(2)}) %copy-start.10) | copy-done | bytes 4632
  48.0 0.0 copy-done.15
  48.0 0.7 %copy.30.rows = s32[32,1]{1,0:T(8,128)} copy(s32[32,1]{0,1:T(1,128)S(1)} %bitcast.31) | data formatting | bytes 256 | tf_op jit(solution)/shard_map/concatenate | solution.py:277
  48.7 8.5 %shard_map.164 = f32[36,256]{1,0:T(8,128)} custom-call(f32[36,256]{1,0:T(8,128)} %copy-done.5, f32[16,2,36]{2,1,0:T(2,128)} %copy-done.10, s32[32,1]{1,0:T(8,128)} %copy.30.rows), custom_call_target="tpu_custom_call" | custom-call | tf_op jit(solution)/shard_map/pallas_call | solution.py:332
  57.2 1.4 %copy.39 = f32[36,256]{1,0:T(8,128)} copy(f32[36,256]{1,0:T(8,128)} %shard_map.164) | data formatting | bytes 73728
  (4 shorter events, 0.1 us)
Async XLA Ops:
  5.0 0.7 %copy-start.13 = (bf16[256,36]{0,1:T(8,128)(2,1)S(1)}, bf16[256,36]{0,1:T(8,128)(2,1)}, u32[]{:S(2)}) copy-start(bf16[256,36]{0,1:T(8,128)(2,1)} %param.18) | copy-start | bytes 55300
  7.8 1.0 %copy-start.12 = (bf16[36,36,36]{2,1,0:T(8,128)(2,1)S(1)}, bf16[36,36,36]{2,1,0:T(8,128)(2,1)}, u32[]{:S(2)}) copy-start(bf16[36,36,36]{2,1,0:T(8,128)(2,1)} %param.19) | copy-start | bytes 279940
  9.1 0.7 %copy-start.14 = (s32[16]{0:T(128)S(1)}, s32[16]{0:T(128)}, u32[]{:S(2)}) copy-start(s32[16]{0:T(128)} %param.21) | copy-start | bytes 196
  9.1 1.4 %copy-start = (bf16[2,256,128]{2,1,0:T(8,128)(2,1)S(1)}, bf16[2,256,128]{2,1,0:T(8,128)(2,1)}, u32[]{:S(2)}) copy-start(bf16[2,256,128]{2,1,0:T(8,128)(2,1)} %constant.25.clone.spread_b) | copy-start | bytes 393220
  9.1 1.4 %copy-start.1 = (bf16[2,256,128]{2,1,0:T(8,128)(2,1)S(1)}, bf16[2,256,128]{2,1,0:T(8,128)(2,1)}, u32[]{:S(2)}) copy-start(bf16[2,256,128]{2,1,0:T(8,128)(2,1)} %constant.26.clone.spread_a) | copy-start | bytes 393220
  9.1 1.4 %copy-start.2 = (bf16[256,256]{1,0:T(8,128)(2,1)S(1)}, bf16[256,256]{1,0:T(8,128)(2,1)}, u32[]{:S(2)}) copy-start(bf16[256,256]{1,0:T(8,128)(2,1)} %constant.29.clone.mask_two) | copy-start | bytes 393220
  9.1 1.4 %copy-start.3 = (bf16[256,256]{1,0:T(8,128)(2,1)S(1)}, bf16[256,256]{1,0:T(8,128)(2,1)}, u32[]{:S(2)}) copy-start(bf16[256,256]{1,0:T(8,128)(2,1)} %constant.30.clone.mask_three) | copy-start | bytes 393220
  9.2 1.4 %copy-start.4 = (bf16[36,1536]{1,0:T(8,128)(2,1)S(1)}, bf16[36,1536]{1,0:T(8,128)(2,1)}, u32[]{:S(2)}) copy-start(bf16[36,1536]{1,0:T(8,128)(2,1)} %constant.32.clone.second) | copy-start | bytes 331780
  9.2 1.4 %copy-start.6 = (f32[40,256]{1,0:T(8,128)S(1)}, f32[40,256]{1,0:T(8,128)}, u32[]{:S(2)}) copy-start(f32[40,256]{1,0:T(8,128)} %constant.33.clone.first_rows) | copy-start | bytes 122884
  9.2 1.4 %copy-start.7 = (bf16[40,256]{1,0:T(8,128)(2,1)S(1)}, bf16[40,256]{1,0:T(8,128)(2,1)}, u32[]{:S(2)}) copy-start(bf16[40,256]{1,0:T(8,128)(2,1)} %constant.27.clone.both_two) | copy-start | bytes 61444
  9.2 1.4 %copy-start.8 = (bf16[40,256]{1,0:T(8,128)(2,1)S(1)}, bf16[40,256]{1,0:T(8,128)(2,1)}, u32[]{:S(2)}) copy-start(bf16[40,256]{1,0:T(8,128)(2,1)} %constant.28.clone.both_three) | copy-start | bytes 61444
  9.2 1.4 %copy-start.9 = (bf16[36,256]{1,0:T(8,128)(2,1)S(1)}, bf16[36,256]{1,0:T(8,128)(2,1)}, u32[]{:S(2)}) copy-start(bf16[36,256]{1,0:T(8,128)(2,1)} %constant.31.clone.first) | copy-start | bytes 55300
  9.2 1.4 %copy-start.11 = (s32[16]{0:T(128)S(1)}, s32[16]{0:T(128)}, u32[]{:S(2)}) copy-start(s32[16]{0:T(128)} %slot_ref.1) | copy-start | bytes 196
  9.5 38.5 %copy-start.15 = (s32[1,32]{1,0:T(1,128)S(1)}, s32[1,32]{1,0:T(1,128)}, u32[]{:S(2)}) copy-start(s32[1,32]{1,0:T(1,128)} %param.20) | copy-start | bytes 388
  46.8 0.6 %copy-start.5 = (f32[36,256]{1,0:T(8,128)}, f32[36,256]{1,0:T(8,128)S(1)}, u32[]{:S(2)}) copy-start(f32[36,256]{1,0:T(8,128)S(1)} %get-tuple-element.7.rates) | copy-start | bytes 110596
  47.4 0.6 %copy-start.10 = (f32[16,2,36]{2,1,0:T(2,128)}, f32[16,2,36]{2,1,0:T(2,128)S(1)}, u32[]{:S(2)}) copy-start(f32[16,2,36]{2,1,0:T(2,128)S(1)} %get-tuple-element.8.sent) | copy-start | bytes 13828

commit v3 on v2

--- a/solution.py
+++ b/solution.py
@@ -143,7 +143,7 @@
     count, cap, slot_ref, live, outgoing, near, partner, force, near_freq, partner_freq,
     near_col, slot_row, spread_b, spread_a, both_two, both_three, mask_two, mask_three,
     first, second, first_rows, rates, by_slot, arrived, two_all, three_all, y_all, z_all,
-    w_first, w_second, w_third, near_acc, send_sem, recv_sem,
+    w_first, w_second, w_third, near_acc, far_all, x_all, send_sem, recv_sem,
 ):
     slots = near.shape[0]
     me, _ = peers(count)
@@ -174,14 +174,17 @@
     def fill(t, carry):
         far = arrived[slot_ref[t] // cap, slot_ref[t] % cap]
         w_third[t] = jnp.broadcast_to(far[:, 2 * NB : 2 * NB + 1].astype(F32), (ROWS, WIDE))
-        for group in range(GROUPS):
-            for part in range(2):
-                rows = pl.ds(part * ROWS, ROWS)
-                tile = force[part, pl.ds(group * WIDE, WIDE), :]
-                y_all[t, group, rows] = nt(far, tile).astype(BF16)
+        far_all[t] = far.astype(F32)
         return carry
 
     lax.fori_loop(0, slots, fill, 0, unroll=2)
+    fars = far_all[...].reshape(slots * ROWS, 128).astype(BF16)
+    for group in range(GROUPS):
+        for part in range(2):
+            made = nt(fars, force[part, pl.ds(group * WIDE, WIDE), :])
+            y_all[:, group, pl.ds(part * ROWS, ROWS), :] = made.reshape(
+                slots, ROWS, WIDE
+            ).astype(BF16)
     lane = lax.broadcasted_iota(jnp.int32, (2 * ROWS, 128), 1)
     column = lax.broadcasted_iota(jnp.int32, (1, 128), 1)
     wide_lane = lax.broadcasted_iota(jnp.int32, (1, WIDE), 1) % 128
@@ -190,8 +193,9 @@
     def one(t, far_cols):
         two = two_all[t]
         three = three_all[t]
+        made = nn(y_all[t].reshape(GROUPS * 2 * ROWS, WIDE), two)
         for group in range(GROUPS):
-            part = nn(y_all[t, group], two)
+            part = made[group * 2 * ROWS : (group + 1) * 2 * ROWS]
             real = part[:ROWS, :WIDE] - part[ROWS:, WIDE:]
             imag = part[:ROWS, WIDE:] + part[ROWS:, :WIDE]
             z_all[group] = jnp.concatenate([real, imag], 0)
@@ -215,7 +219,10 @@
                         jnp.where(lane < 80, pieces[1], jnp.where(lane < 120, pieces[2], 0.0)),
                     )
                 )
-            part = nn(jnp.concatenate(tiles, 1).astype(BF16), three)
+            x_all[group] = jnp.concatenate(tiles, 1).astype(BF16)
+        made = nn(x_all[...].reshape(GROUPS * 2 * ROWS, WIDE), three)
+        for group in range(GROUPS):
+            part = made[group * 2 * ROWS : (group + 1) * 2 * ROWS]
             real = part[:ROWS, :WIDE] - part[ROWS:, WIDE:]
             imag = part[:ROWS, WIDE:] + part[ROWS:, :WIDE]
             power = real * real + imag * imag
@@ -310,6 +317,8 @@
             pltpu.VMEM((slots, GROUPS * WIDE), F32),
             pltpu.VMEM((slots, ROWS, WIDE), F32),
             pltpu.VMEM((slots, WIDE), F32),
+            pltpu.VMEM((slots, ROWS, 128), F32),
+            pltpu.VMEM((GROUPS, 2 * ROWS, WIDE), BF16),
             pltpu.SemaphoreType.DMA((count,)),
             pltpu.SemaphoreType.DMA((count,)),
         ],

time: 59 us -> 52 us (0.88)
  Pallas kernels: 44.7 us -> 37.7 us
    pallas_call x1, Pallas kernels: 36.2 us -> 29.2 us  [on_device(): pl.pallas_call(functools.partial(contract_kernel, count, cap), out_shape=...]
where the time goes in v3:
time: 52 us; the launch traced here: 51.6 us
  Pallas kernels  37.7 us (73%)
  local copies, waits for them, and re-layouts  11.2 us (22%)
  other arithmetic  1.7 us (3%)
  between operations  0.96 us (2%)
    pallas_call x1, Pallas kernels, on_device(): pl.pallas_call(functools.partial(contract_kernel, count, cap), out_shape=...  29.2 us
    pallas_call x1, Pallas kernels, on_device(): pl.pallas_call(functools.partial(finish_kernel, count), out_shape=jax.Sha...  8.47 us
    unnamed x35, local copies, waits for them, and re-layouts  6.31 us
    reshape x1, local copies, waits for them, and re-layouts, on_device(): vecs = take(eigvec, wanted).reshape(-1, 2, NB, NB)  1.64 us
    gather x2, local copies, waits for them, and re-layouts, take(): return array.at[rows].get(mode='promise_in_bounds')  1.42 us

profile of v3, /device:TPU:0, one launch (start us, length us, event | category | flops | bytes accessed | tf_op | source)
XLA Modules:
  0.0 51.6 jit_solution(109515588987083147)
XLA Ops:
  0.0 0.8 %fusion.9 = s32[64]{0:T(128)S(1)} fusion(s32[16,1]{0,1:T(1,128)} %bitcast.32, s32[16,1]{0,1:T(1,128)} %bitcast.28, s32[32,1]{0,1:T(1,128)} %bitcast.30), kind=kLoop, calls=%fused_computation.20 | loop fusion | flops 320 | bytes 512 | tf_op jit(solution)/shard_map/select_n | solution.py:274
  0.8 1.8 %copy.22 = bf16[256,2592]{1,0:T(8,128)(2,1)S(1)} copy(bf16[256,2592]{0,1:T(8,128)(2,1)} %param.17) | data formatting | bytes 2654208 | tf_op args[0]
  2.6 0.8 %gather_fusion = bf16[64,2592]{1,0:T(8,128)(2,1)S(1)} fusion(bf16[256,2592]{1,0:T(8,128)(2,1)S(1)} %copy.22, s32[1024]{0:T(1024)S(1)} %pad_clamp_fusion), kind=kCustom, calls=%fused_computation | custom fusion | bytes 663808 | tf_op jit(solution)/shard_map/gather | solution.py:274
  3.4 1.6 %reshape.153 = bf16[64,2,36,36]{3,2,1,0:T(8,128)(2,1)S(1)} reshape(bf16[64,2592]{1,0:T(8,128)(2,1)S(1)} %gather_fusion) | data formatting | bytes 663552 | tf_op jit(solution)/shard_map/reshape | solution.py:285
  5.0 0.0 copy-start.13
  5.0 0.1 slice_bitcast_fusion.1
  5.1 0.6 %copy-done.13 = bf16[256,36]{0,1:T(8,128)(2,1)S(1)} copy-done((bf16[256,36]{0,1:T(8,128)(2,1)S(1)}, bf16[256,36]{0,1:T(8,128)(2,1)}, u32[]{:S(2)}) %copy-start.13) | copy-done | bytes 18456
  5.7 0.1 copy.26
  5.9 0.6 %gather_fusion.1 = bf16[64,36]{1,0:T(8,128)(2,1)S(1)} fusion(bf16[256,36]{1,0:T(8,128)(2,1)S(1)} %copy.26, s32[1024]{0:T(1024)S(1)} %pad_clamp_fusion), kind=kCustom, calls=%fused_computation.1 | custom fusion | bytes 9472 | tf_op jit(solution)/shard_map/gather | solution.py:274
  6.5 0.5 %copy.28 = bf16[64,36,1]{2,1,0:T(8,128)(2,1)S(1)} copy(bf16[64,36,1]{1,0,2:T(8,128)(2,1)S(1)} %bitcast.27) | data formatting | bytes 9216 | tf_op jit(solution)/shard_map/broadcast_in_dim | solution.py:287
  7.0 0.8 %fusion.8 = bf16[64,40,128]{2,1,0:T(8,128)(2,1)S(1)} fusion(bf16[64,36,1]{2,1,0:T(8,128)(2,1)S(1)} %copy.28, bf16[64,36,36]{2,1,0:T(8,128)(2,1)S(1)} %get-tuple-element.10, bf16[64,36,36]{2,1,0:T(8,128)(2,1)S(1)} %get-tuple-element.9), kind=kLoop, calls=%fused_computation.13 | loop fusion | flops 4915200 | bytes 991744 | tf_op jit(solution)/shard_map/concatenate | solution.py:287
  7.8 0.0 copy-start.12
  7.9 0.9 %copy-done.12 = bf16[36,36,36]{2,1,0:T(8,128)(2,1)S(1)} copy-done((bf16[36,36,36]{2,1,0:T(8,128)(2,1)S(1)}, bf16[36,36,36]{2,1,0:T(8,128)(2,1)}, u32[]{:S(2)}) %copy-start.12) | copy-done | bytes 93336
  8.8 0.1 pad.21
  8.9 0.1 pad.22
  9.0 0.1 bitcast_negate_fusion
  9.1 0.0 copy-start.14
  9.1 0.0 copy-start
  9.1 0.0 copy-start.1
  9.1 0.0 copy-start.2
  9.1 0.0 copy-start.3
  9.2 0.0 copy-start.4
  9.2 0.0 copy-start.6
  9.2 0.0 copy-start.7
  9.2 0.0 copy-start.8
  9.2 0.0 copy-start.9
  9.2 0.0 copy-start.11
  9.2 0.2 pad_bitcast_fusion
  9.5 0.1 pad_maximum_fusion.force
  9.5 0.0 copy-start.15
  9.6 0.2 copy-done.14
  9.8 0.1 copy.29.near_col
  10.5 0.0 copy-done
  10.5 0.0 copy-done.1
  10.5 0.0 copy-done.2
  10.5 0.0 copy-done.3
  10.5 0.0 copy-done.4
  10.5 0.0 copy-done.6
  10.5 0.0 copy-done.7
  10.6 0.0 copy-done.8
  10.6 0.0 copy-done.9
  10.6 0.0 copy-done.11
  10.6 29.2 %shard_map.163 = (f32[36,256]{1,0:T(8,128)S(1)}, f32[16,2,36]{2,1,0:T(2,128)S(1)}) custom-call(s32[16]{0:T(128)S(1)} %copy-done.11, s32[1]{0:T(128)S(6)} %copy.38.live, bf16[16,2,40,128]{3,2,1,0:T(8,128)(2,1)S(1)} %bitcast.23, bf16[16,40,128]{2,1,0:T(8,128)(2,1)S(1)} %get-tuple-element.12.near, bf16[16,40,128]{2,1,0:T(8,128)(2,1)S(1)} %get-tuple-element.11.partner, ...), custom_call_target="tpu_custom_call" | custom-call | tf_op jit(solution)/shard_map/pallas_call | solution.py:302
  39.8 0.0 copy-start.5
  39.8 0.6 %copy-done.5 = f32[36,256]{1,0:T(8,128)} copy-done((f32[36,256]{1,0:T(8,128)}, f32[36,256]{1,0:T(8,128)S(1)}, u32[]{:S(2)}) %copy-start.5) | copy-done | bytes 36888
  40.4 0.0 copy-start.10
  40.4 0.6 %copy-done.10 = f32[16,2,36]{2,1,0:T(2,128)} copy-done((f32[16,2,36]{2,1,0:T(2,128)}, f32[16,2,36]{2,1,0:T(2,128)S(1)}, u32[]{:S(2)}) %copy-start.10) | copy-done | bytes 4632
  41.0 0.0 copy-done.15
  41.0 0.7 %copy.30.rows = s32[32,1]{1,0:T(8,128)} copy(s32[32,1]{0,1:T(1,128)S(1)} %bitcast.31) | data formatting | bytes 256 | tf_op jit(solution)/shard_map/concatenate | solution.py:284
  41.7 8.5 %shard_map.164 = f32[36,256]{1,0:T(8,128)} custom-call(f32[36,256]{1,0:T(8,128)} %copy-done.5, f32[16,2,36]{2,1,0:T(2,128)} %copy-done.10, s32[32,1]{1,0:T(8,128)} %copy.30.rows), custom_call_target="tpu_custom_call" | custom-call | tf_op jit(solution)/shard_map/pallas_call | solution.py:341
  50.2 1.4 %copy.39 = f32[36,256]{1,0:T(8,128)} copy(f32[36,256]{1,0:T(8,128)} %shard_map.164) | data formatting | bytes 73728
  (4 shorter events, 0.1 us)
Async XLA Ops:
  5.0 0.7 %copy-start.13 = (bf16[256,36]{0,1:T(8,128)(2,1)S(1)}, bf16[256,36]{0,1:T(8,128)(2,1)}, u32[]{:S(2)}) copy-start(bf16[256,36]{0,1:T(8,128)(2,1)} %param.18) | copy-start | bytes 55300
  7.8 1.0 %copy-start.12 = (bf16[36,36,36]{2,1,0:T(8,128)(2,1)S(1)}, bf16[36,36,36]{2,1,0:T(8,128)(2,1)}, u32[]{:S(2)}) copy-start(bf16[36,36,36]{2,1,0:T(8,128)(2,1)} %param.19) | copy-start | bytes 279940
  9.1 0.7 %copy-start.14 = (s32[16]{0:T(128)S(1)}, s32[16]{0:T(128)}, u32[]{:S(2)}) copy-start(s32[16]{0:T(128)} %param.21) | copy-start | bytes 196
  9.1 1.4 %copy-start = (bf16[2,256,128]{2,1,0:T(8,128)(2,1)S(1)}, bf16[2,256,128]{2,1,0:T(8,128)(2,1)}, u32[]{:S(2)}) copy-start(bf16[2,256,128]{2,1,0:T(8,128)(2,1)} %constant.25.clone.spread_b) | copy-start | bytes 393220
  9.1 1.4 %copy-start.1 = (bf16[2,256,128]{2,1,0:T(8,128)(2,1)S(1)}, bf16[2,256,128]{2,1,0:T(8,128)(2,1)}, u32[]{:S(2)}) copy-start(bf16[2,256,128]{2,1,0:T(8,128)(2,1)} %constant.26.clone.spread_a) | copy-start | bytes 393220
  9.1 1.4 %copy-start.2 = (bf16[256,256]{1,0:T(8,128)(2,1)S(1)}, bf16[256,256]{1,0:T(8,128)(2,1)}, u32[]{:S(2)}) copy-start(bf16[256,256]{1,0:T(8,128)(2,1)} %constant.29.clone.mask_two) | copy-start | bytes 393220
  9.1 1.4 %copy-start.3 = (bf16[256,256]{1,0:T(8,128)(2,1)S(1)}, bf16[256,256]{1,0:T(8,128)(2,1)}, u32[]{:S(2)}) copy-start(bf16[256,256]{1,0:T(8,128)(2,1)} %constant.30.clone.mask_three) | copy-start | bytes 393220
  9.2 1.4 %copy-start.4 = (bf16[36,1536]{1,0:T(8,128)(2,1)S(1)}, bf16[36,1536]{1,0:T(8,128)(2,1)}, u32[]{:S(2)}) copy-start(bf16[36,1536]{1,0:T(8,128)(2,1)} %constant.32.clone.second) | copy-start | bytes 331780
  9.2 1.4 %copy-start.6 = (f32[40,256]{1,0:T(8,128)S(1)}, f32[40,256]{1,0:T(8,128)}, u32[]{:S(2)}) copy-start(f32[40,256]{1,0:T(8,128)} %constant.33.clone.first_rows) | copy-start | bytes 122884
  9.2 1.4 %copy-start.7 = (bf16[40,256]{1,0:T(8,128)(2,1)S(1)}, bf16[40,256]{1,0:T(8,128)(2,1)}, u32[]{:S(2)}) copy-start(bf16[40,256]{1,0:T(8,128)(2,1)} %constant.27.clone.both_two) | copy-start | bytes 61444
  9.2 1.4 %copy-start.8 = (bf16[40,256]{1,0:T(8,128)(2,1)S(1)}, bf16[40,256]{1,0:T(8,128)(2,1)}, u32[]{:S(2)}) copy-start(bf16[40,256]{1,0:T(8,128)(2,1)} %constant.28.clone.both_three) | copy-start | bytes 61444
  9.2 1.4 %copy-start.9 = (bf16[36,256]{1,0:T(8,128)(2,1)S(1)}, bf16[36,256]{1,0:T(8,128)(2,1)}, u32[]{:S(2)}) copy-start(bf16[36,256]{1,0:T(8,128)(2,1)} %constant.31.clone.first) | copy-start | bytes 55300
  9.2 1.4 %copy-start.11 = (s32[16]{0:T(128)S(1)}, s32[16]{0:T(128)}, u32[]{:S(2)}) copy-start(s32[16]{0:T(128)} %slot_ref.1) | copy-start | bytes 196
  9.5 31.5 %copy-start.15 = (s32[1,32]{1,0:T(1,128)S(1)}, s32[1,32]{1,0:T(1,128)}, u32[]{:S(2)}) copy-start(s32[1,32]{1,0:T(1,128)} %param.20) | copy-start | bytes 388
  39.8 0.6 %copy-start.5 = (f32[36,256]{1,0:T(8,128)}, f32[36,256]{1,0:T(8,128)S(1)}, u32[]{:S(2)}) copy-start(f32[36,256]{1,0:T(8,128)S(1)} %get-tuple-element.7.rates) | copy-start | bytes 110596
  40.4 0.6 %copy-start.10 = (f32[16,2,36]{2,1,0:T(2,128)}, f32[16,2,36]{2,1,0:T(2,128)S(1)}, u32[]{:S(2)}) copy-start(f32[16,2,36]{2,1,0:T(2,128)S(1)} %get-tuple-element.8.sent) | copy-start | bytes 13828
